TPU v7x, 512 devices: a whole 4x8x8 slice. The times are simulated.
512 devices in a mesh: doc: 32 (over y, x), seq: 16 (over z, core).
Axes of the slice: x: 4, y: 8, z: 8, core: 2. Of those that a mesh axis runs over, the one named last changes fastest.
Arguments:
- tokens: bfloat16 [131072, 1024], P(('doc', 'seq')), parts along dimension 0, may hold values from -8 to 8
- bottom_qkv: bfloat16 [1024, 3072], P('seq'), may hold values from -1 to 1
- bottom_out: bfloat16 [1024, 1024], P('seq'), may hold values from -0.5 to 0.5
- top_qkv: bfloat16 [1024, 3, 1024], P(None, None, 'seq'), may hold values from -1 to 1
- top_out: bfloat16 [1024, 1024], P('seq'), may hold values from -0.5 to 0.5
- cross_query: bfloat16 [1024, 1024], P('seq'), may hold values from -1 to 1
- cross_kv: bfloat16 [1024, 2, 1024], P(None, None, 'seq'), may hold values from -1 to 1
- cross_out: bfloat16 [1024, 1024], P('seq'), may hold values from -0.5 to 0.5
Outputs:
- encoded: bfloat16 [131072, 1024], P(('doc', 'seq')), parts along dimension 0
There are 32 independent parts, one for each index of `doc`. A program takes and returns all parts, laid end to end along the dimension named above; an argument that names none is the same for every part. Nothing has to cross between parts.
All inputs are finite; a program needn't handle non-finite values.
Results may differ from a plain program's by a relative error of at most 0.013.
Values may be sent and summed in bfloat16 or wider, within the bound.
A program may use at most 64 MiB of HBM per device.

v0:
```python
import math
import jax
import jax.numpy as jnp
from jax import lax
from jax.sharding import PartitionSpec as P

H = 16
W = 512
POOL = 32
EPS = 1e-06


def padded(cells, sides, width):
    for axis, dim in sides:
        count = lax.axis_size(axis)
        ends = count - 1
        head = lax.slice_in_dim(cells, 0, width, axis=dim)
        tail = lax.slice_in_dim(cells, cells.shape[dim] - width, cells.shape[dim], axis=dim)
        cells = jnp.concatenate(
            [
                lax.ppermute(tail, axis, [(i, (i + 1) % count) for i in range(ends)]),
                cells,
                lax.ppermute(head, axis, [((i + 1) % count, i) for i in range(ends)]),
            ],
            axis=dim,
        )
    return cells


def normed(values_in):
    values_in = values_in.astype(jnp.float32)
    return (
        values_in * lax.rsqrt(jnp.mean(values_in * values_in, axis=-1, keepdims=True) + EPS)
    ).astype(jnp.bfloat16)


def window_mask(first_tok, tok_count, half_win, total_tok):
    query_pos = first_tok + jnp.arange(tok_count, dtype=jnp.int32)
    key_pos = first_tok - half_win + jnp.arange(tok_count + 2 * half_win, dtype=jnp.int32)
    offsets = key_pos[None, :] - query_pos[:, None]
    inside = (key_pos[None, :] >= 0) & (key_pos[None, :] < total_tok)
    return (offsets >= -half_win) & (offsets < half_win) & inside


def attend(queries, key_mat, value_mat, allowed, head_count):
    row_count = queries.shape[0]
    key_count = key_mat.shape[0]
    head_width = queries.shape[1] // head_count
    score_scale = 1.0 / math.sqrt(head_width)
    split_q = queries.reshape(row_count, head_count, head_width).transpose(1, 0, 2)
    split_k = key_mat.reshape(key_count, head_count, head_width).transpose(1, 0, 2)
    split_v = value_mat.reshape(key_count, head_count, head_width).transpose(1, 0, 2)

    def one_head(operands):
        query_h, key_h, value_h = operands
        scores = jnp.dot(query_h, key_h.T, preferred_element_type=jnp.float32) * score_scale
        if allowed is not None:
            scores = jnp.where(allowed, scores, -1e30)
        row_peak = jnp.max(scores, axis=1, keepdims=True)
        expo = jnp.exp(scores - row_peak)
        row_total = jnp.sum(expo, axis=1, keepdims=True)
        mixture = (
            jnp.dot(expo.astype(jnp.bfloat16), value_h, preferred_element_type=jnp.float32)
            / row_total
        )
        return mixture.astype(jnp.bfloat16)

    merged = lax.map(one_head, (split_q, split_k, split_v))
    return merged.transpose(1, 0, 2).reshape(row_count, head_count * head_width)


def fold_rows(operand, shard_rows):
    return jnp.dot(operand, shard_rows, preferred_element_type=jnp.float32)


def local(tokens, bottom_qkv, bottom_out, top_qkv, top_out, cross_query, cross_kv, cross_out):
    tok_count, model_width = tokens.shape
    devices_seq = lax.axis_size("seq")
    local_heads = H // devices_seq
    half_win = W // 2
    total_tok = tok_count * devices_seq
    first_tok = lax.axis_index("seq") * tok_count
    normed_tok = normed(tokens)
    project = fold_rows(normed_tok, lax.all_gather(bottom_qkv, "seq", axis=0, tiled=True))
    project = project.astype(jnp.bfloat16)
    queries = project[:, :model_width]
    key_vals = padded(project[:, model_width:], (("seq", 0),), half_win)
    allowed = window_mask(first_tok, tok_count, half_win, total_tok)
    attended = attend(queries, key_vals[:, :model_width], key_vals[:, model_width:], allowed, H)
    out_sum = fold_rows(attended, lax.all_gather(bottom_out, "seq", axis=0, tiled=True))
    lower_tok = (tokens.astype(jnp.float32) + out_sum).astype(jnp.bfloat16)
    pooled = jnp.mean(
        lower_tok.astype(jnp.float32).reshape(tok_count // POOL, POOL, model_width), axis=1
    ).astype(jnp.bfloat16)
    all_units = lax.all_gather(pooled, "seq", axis=0, tiled=True)
    unit_norm = normed(all_units)
    top_q = jnp.dot(unit_norm, top_qkv[:, 0, :], preferred_element_type=jnp.float32).astype(
        jnp.bfloat16
    )
    top_k = jnp.dot(unit_norm, top_qkv[:, 1, :], preferred_element_type=jnp.float32).astype(
        jnp.bfloat16
    )
    top_v = jnp.dot(unit_norm, top_qkv[:, 2, :], preferred_element_type=jnp.float32).astype(
        jnp.bfloat16
    )
    top_att = attend(top_q, top_k, top_v, None, local_heads)
    head_term = jnp.dot(top_att, top_out, preferred_element_type=jnp.float32)
    head_total = lax.psum(head_term.astype(jnp.bfloat16), "seq").astype(jnp.float32)
    top_units = (all_units.astype(jnp.float32) + head_total).astype(jnp.bfloat16)
    upper_norm = normed(top_units)
    part_keys = jnp.dot(upper_norm, cross_kv[:, 0, :], preferred_element_type=jnp.float32).astype(
        jnp.bfloat16
    )
    part_vals = jnp.dot(upper_norm, cross_kv[:, 1, :], preferred_element_type=jnp.float32).astype(
        jnp.bfloat16
    )
    stacked = jnp.concatenate([part_keys, part_vals], axis=1)
    gathered = lax.all_gather(stacked, "seq", axis=1, tiled=True)
    unit_count = gathered.shape[0]
    arranged = gathered.reshape(unit_count, devices_seq, 2, part_keys.shape[1])
    cross_keys = arranged[:, :, 0, :].reshape(unit_count, model_width)
    cross_vals = arranged[:, :, 1, :].reshape(unit_count, model_width)
    lower_norm = normed(lower_tok)
    query_acc = fold_rows(lower_norm, lax.all_gather(cross_query, "seq", axis=0, tiled=True))
    cross_q = query_acc.astype(jnp.bfloat16)
    cross_att = attend(cross_q, cross_keys, cross_vals, None, H)
    cross_sum = fold_rows(cross_att, lax.all_gather(cross_out, "seq", axis=0, tiled=True))
    return (lower_tok.astype(jnp.float32) + cross_sum).astype(jnp.bfloat16)


def solution(mesh):
    in_specs = (
        P(("doc", "seq"), None),
        P("seq", None),
        P("seq", None),
        P(None, None, "seq"),
        P("seq", None),
        P("seq", None),
        P(None, None, "seq"),
        P("seq", None),
    )
    out_specs = P(("doc", "seq"), None)
    return jax.shard_map(local, mesh=mesh, in_specs=in_specs, out_specs=out_specs, check_vma=False)
```

profile of v0, /device:TPU:1, one launch (start us, length us, event | category | flops | bytes accessed | tf_op | source)
XLA Modules:
  0.0 322.5 jit_solution(8568578363218023782)
XLA Ops:
  9.3 55.6 %all-gather.5.cloned.1.call-done = bf16[1024,3072]{1,0:T(8,128)(2,1)} async-done(((bf16[64,3072]{1,0:T(8,128)(2,1)}), bf16[1024,3072]{1,0:T(8,128)(2,1)}) %all-gather.5.cloned.1.call-update) | async-done | bytes 6291472 | tf_op jit(solution)/shard_map/all_gather | solution.py:84
  64.9 4.8 %convolution_convert_fusion = bf16[256,3072]{1,0:T(8,128)(2,1)S(1)} fusion(bf16[1024,3072]{1,0:T(8,128)(2,1)} %all-gather.5.cloned.1.call-done, bf16[256,1024]{1,0:T(8,128)(2,1)} %param.12, f32[256]{0:T(256)S(1)} %add_rsqrt_fusion.1), kind=kOutput, calls=%fused_computation.40 | convolution fusion | flops 1612185600 | bytes 8389632 | tf_op jit(solution)/shard_map/dot_general | solution.py:73
  69.8 2.7 collective-permute-start
  72.5 2.6 collective-permute-start.1
  76.3 10.8 %collective-permute-done = bf16[256,2048]{1,0:T(8,128)(2,1)} collective-permute-done((bf16[256,2048]{1,0:T(8,128)(2,1)S(1)}, bf16[256,2048]{1,0:T(8,128)(2,1)}, u32[]{:S(2)}, u32[]{:S(2)}) %collective-permute-start) | collective-permute-done | bytes 1048608 | tf_op jit(solution)/shard_map/ppermute | solution.py:21
  87.1 6.1 %collective-permute-done.1 = bf16[256,2048]{1,0:T(8,128)(2,1)} collective-permute-done((bf16[256,2048]{1,0:T(8,128)(2,1)S(1)}, bf16[256,2048]{1,0:T(8,128)(2,1)}, u32[]{:S(2)}, u32[]{:S(2)}) %collective-permute-start.1) | collective-permute-done | bytes 1048608 | tf_op jit(solution)/shard_map/ppermute | solution.py:23
  93.2 1.7 pad_maximum_fusion
  95.2 1.6 copy.16
  97.6 33.1 %while.26 = (s32[]{:T(128)}, bf16[16,256,64]{1,2,0:T(8,128)(2,1)S(1)}, bf16[16,256,64]{1,2,0:T(8,128)(2,1)}, bf16[16,768,64]{1,2,0:T(8,128)(2,1)}, bf16[16,768,6...) while((s32[]{:T(128)}, ...), condition=%wide.region_4.5_spmd.clone, body=%wide.region_1.4_spmd.clone.sunk | while | flops 52723200 | bytes 2633565 | solution.py:68
  97.6 1.4 fusion.111
  99.7 1.4 fusion.111
  101.8 1.4 fusion.111
  103.8 1.4 fusion.111
  105.9 1.4 fusion.111
  108.0 1.4 fusion.111
  110.0 1.4 fusion.111
  112.1 1.4 fusion.111
  114.1 1.4 fusion.111
  116.2 1.4 fusion.111
  118.3 1.4 fusion.111
  120.3 1.4 fusion.111
  122.4 1.4 fusion.111
  124.5 1.4 fusion.111
  128.6 1.4 fusion.111
  130.7 2.4 bitcast_reduce_fusion
  133.1 16.1 %all_gather.21 = bf16[128,1024]{1,0:T(8,128)(2,1)S(1)} all-gather(bf16[8,1024]{1,0:T(8,128)(2,1)S(1)} %multiply_convert_fusion.2), channel_id=1, replica_groups=mesh['doc'=32,'seq'=16] {'seq'}, dimensions={0}, use_global_device_ids=true | all-gather | bytes 278528 | tf_op jit(solution)/shard_map/all_gather | solution.py:95
  152.4 2.3 convolution_convert_fusion.1
  154.9 112.5 %all-reduce.2.cloned.1.call-done = bf16[128,1024]{1,0:T(8,128)(2,1)} async-done(((bf16[128,1024]{1,0:T(8,128)(2,1)}), bf16[128,1024]{1,0:T(8,128)(2,1)}) %all-reduce.2.cloned.1.call-update) | async-done | bytes 262160 | tf_op jit(solution)/shard_map/psum | solution.py:108
  271.1 16.9 %all_gather.22 = bf16[128,2048]{0,1:T(8,128)(2,1)S(1)} all-gather(bf16[128,128]{0,1:T(8,128)(2,1)S(1)} %pad_maximum_fusion.1), channel_id=1, replica_groups=mesh['doc'=32,'seq'=16] {'seq'}, dimensions={1}, use_global_device_ids=true | all-gather | bytes 557056 | tf_op jit(solution)/shard_map/all_gather | solution.py:118
  288.7 7.1 %while.25 = (s32[]{:T(128)}, bf16[16,256,64]{1,2,0:T(8,128)(2,1)S(1)}, bf16[16,256,64]{1,2,0:T(8,128)(2,1)S(1)}, bf16[16,128,64]{2,1,0:T(8,128)(2,1)S(1)}, bf16[16,128,64]{2,1,0:T(8,128)(2,1)S(1)}, /*index=5*/s32[]{:T(128)}) while((s32[]{:T(128)}, bf16[16,256,64]{1,2,0:T(8,128)(2,1)S(1)}, bf16[16,256,64]{1,2,0:T(8,128)(2,1)S(1)}, ...), condition=%wide.region_15.16_spmd, body=%wide.region_12.15_spmd.sunk | while | flops 8617474 | bytes 531525 | solution.py:68
  295.8 17.0 %all-gather.11.cloned.1.call-done = bf16[1024,1024]{1,0:T(8,128)(2,1)} async-done(((bf16[64,1024]{1,0:T(8,128)(2,1)}), bf16[1024,1024]{1,0:T(8,128)(2,1)}) %all-gather.11.cloned.1.call-update) | async-done | bytes 2097168 | tf_op jit(solution)/shard_map/all_gather | solution.py:127
  312.8 3.1 fusion.37
  (132 shorter events, 31.2 us)
Async XLA Ops:
  6.5 144.0 %copy-start = (bf16[64,1024]{1,0:T(8,128)(2,1)S(1)}, bf16[64,1024]{1,0:T(8,128)(2,1)}, u32[]{:S(2)}) copy-start(bf16[64,1024]{1,0:T(8,128)(2,1)} %param.16) | copy-start | bytes 393220
  6.5 58.4 %all-gather.5.cloned.1.call-start = ((), (), s32[]{:S(2)}) async-start(), calls=%async_computation | async-start | bytes 6684672 | tf_op jit(solution)/shard_map/all_gather | solution.py:84
  7.3 123.4 %all-gather.7.cloned.1.call-start = ((), (), s32[]{:S(2)}) async-start(), calls=%async_computation.1 | async-start | bytes 2228224 | tf_op jit(solution)/shard_map/all_gather | solution.py:90
  8.0 144.4 %all-gather.9.cloned.1.call-start = ((), (), s32[]{:S(2)}) async-start(), calls=%async_computation.2 | async-start | bytes 2228224 | tf_op jit(solution)/shard_map/all_gather | solution.py:124
  69.8 17.2 %collective-permute-start = (bf16[256,2048]{1,0:T(8,128)(2,1)S(1)}, bf16[256,2048]{1,0:T(8,128)(2,1)}, u32[]{:S(2)}, u32[]{:S(2)}) collective-permute-start(bf16[256,2048]{1,0:T(8,128)(2,1)S(1)} %slice.45), channel_id=1, source_target_pairs={{0,1},{1,2},{2,3},{3,4},{4,5},{5,6},{6,7},{7,8},{8,9},{9,10},{10,1... | collective-permute-start | bytes 3145736 | tf_op jit(solution)/shard_map/ppermute | solution.py:21
  72.5 20.7 %collective-permute-start.1 = (bf16[256,2048]{1,0:T(8,128)(2,1)S(1)}, bf16[256,2048]{1,0:T(8,128)(2,1)}, u32[]{:S(2)}, u32[]{:S(2)}) collective-permute-start(bf16[256,2048]{1,0:T(8,128)(2,1)S(1)} %slice.45), channel_id=1, source_target_pairs={{1,0},{2,1},{3,2},{4,3},{5,4},{6,5},{7,6},{8,7},{9,8},{10,9},{11,1... | collective-permute-start | bytes 3145736 | tf_op jit(solution)/shard_map/ppermute | solution.py:23
  75.2 192.3 %all-reduce.2.cloned.1.call-start = ((), (), s32[]{:S(2)}) async-start(), calls=%async_computation.3 | async-start | bytes 524288 | tf_op jit(solution)/shard_map/psum | solution.py:108
  97.6 33.1 %copy-start.1 = (bf16[256,1024]{1,0:T(8,128)(2,1)S(1)}, bf16[256,1024]{1,0:T(8,128)(2,1)}, u32[]{:S(2)}) copy-start(bf16[256,1024]{1,0:T(8,128)(2,1)} %param.12) | copy-start | bytes 1572868
  130.7 18.7 %copy-start.2 = (bf16[1024,3,64]{0,2,1:T(8,128)(2,1)S(1)}, bf16[1024,3,64]{0,2,1:T(8,128)(2,1)}, u32[]{:S(2)}) copy-start(bf16[1024,3,64]{0,2,1:T(8,128)(2,1)} %param.15) | copy-start | bytes 1179652
  151.5 161.3 %all-gather.11.cloned.1.call-start = ((), (), s32[]{:S(2)}) async-start(), calls=%async_computation.4 | async-start | bytes 2228224 | tf_op jit(solution)/shard_map/all_gather | solution.py:127
  152.3 116.3 %copy-start.3 = (bf16[1024,2,64]{0,2,1:T(8,128)(2,1)S(1)}, bf16[1024,2,64]{0,2,1:T(8,128)(2,1)}, u32[]{:S(2)}) copy-start(bf16[1024,2,64]{0,2,1:T(8,128)(2,1)} %param.18) | copy-start | bytes 786436
Sparse Core Ops, SparseCore 0:
  9.5 55.3 all-gather.4
  67.0 41.1 all-gather.6
  110.3 42.0 all-gather.8
  154.6 112.8 all-reduce.1
  269.6 43.1 all-gather.10
where the time goes:
time: 323 us; the launch traced here: 322 us
  waiting for transfers between devices  204 us (63%)
  matrix products  51.4 us (16%)
  blocking collectives  33 us (10%)
  between operations  13.4 us (4%)
  other arithmetic  9.66 us (3%)
  starting transfers between devices  5.46 us (2%)
  local copies, waits for them, and re-layouts  4.62 us (1%)
    psum x1, waiting for transfers between devices, local(): lax.psum(head_term.astype(jnp.bfloat16), 'seq').astype(jnp.float32)  113 us
    all_gather x1, waiting for transfers between devices, local(): lax.all_gather(bottom_qkv, 'seq', axis=0, tiled=True)  55.6 us
    dot_general x33, matrix products, one_head(): jnp.dot(query_h, key_h.T, preferred_element_type=jnp.float32) * score_scale  25.3 us
    all_gather x1, waiting for transfers between devices, local(): lax.all_gather(cross_out, 'seq', axis=0, tiled=True)  17 us
    all_gather x1, blocking collectives, local(): gathered = lax.all_gather(stacked, 'seq', axis=1, tiled=True)  16.9 us
    all_gather x1, blocking collectives, local(): all_units = lax.all_gather(pooled, 'seq', axis=0, tiled=True)  16.1 us
    dot_general x4, matrix products, fold_rows(): return jnp.dot(operand, shard_rows, preferred_element_type=jnp.float32)  12.7 us
    ppermute x1, waiting for transfers between devices, padded(): lax.ppermute(tail, axis, [(i, (i + 1) % count) for i in range(ends)])  10.8 us
  transfers between devices with their start and end apart: 7, of which 6 were waited for; matrix products, arithmetic and copies ran while one was open for 19% of the time, Pallas kernels for 0%

commit v1 on v0

--- a/solution.py
+++ b/solution.py
@@ -8,6 +8,11 @@
 W = 512
 POOL = 32
 EPS = 1e-06
+
+
+def add_all(block, name):
+    pieces = lax.all_gather(block, name)
+    return jnp.sum(pieces, axis=0)
 
 
 def padded(cells, sides, width):
@@ -105,7 +110,7 @@
     )
     top_att = attend(top_q, top_k, top_v, None, local_heads)
     head_term = jnp.dot(top_att, top_out, preferred_element_type=jnp.float32)
-    head_total = lax.psum(head_term.astype(jnp.bfloat16), "seq").astype(jnp.float32)
+    head_total = add_all(head_term.astype(jnp.bfloat16), "seq").astype(jnp.float32)
     top_units = (all_units.astype(jnp.float32) + head_total).astype(jnp.bfloat16)
     upper_norm = normed(top_units)
     part_keys = jnp.dot(upper_norm, cross_kv[:, 0, :], preferred_element_type=jnp.float32).astype(

time: 323 us -> 252 us (0.78)
  waiting for transfers between devices: 204 us -> 132 us
    psum x1 -> x0, waiting for transfers between devices: 113 us -> none  [local(): lax.psum(head_term.astype(jnp.bfloat16), 'seq').astype(jnp.float32)]
    all_gather x0 -> x1, waiting for transfers between devices: none -> 43.4 us  [add_all(): pieces = lax.all_gather(block, name)]
  transfers between devices with their start and end apart: 7 -> 7, of which waited for: 6 -> 5; matrix products, arithmetic and copies ran while one was open for 19% -> 25% of each run, Pallas kernels for 0% -> 0%
where the time goes in v1:
time: 252 us; the launch traced here: 251 us
  waiting for transfers between devices  132 us (52%)
  matrix products  49.5 us (20%)
  blocking collectives  33.3 us (13%)
  between operations  13.4 us (5%)
  other arithmetic  11.9 us (5%)
  starting transfers between devices  5.51 us (2%)
  local copies, waits for them, and re-layouts  4.65 us (2%)
    all_gather x1, waiting for transfers between devices, local(): lax.all_gather(bottom_qkv, 'seq', axis=0, tiled=True)  55.6 us
    all_gather x1, waiting for transfers between devices, add_all(): pieces = lax.all_gather(block, name)  43.4 us
    dot_general x33, matrix products, one_head(): jnp.dot(query_h, key_h.T, preferred_element_type=jnp.float32) * score_scale  25.3 us
    all_gather x1, blocking collectives, local(): gathered = lax.all_gather(stacked, 'seq', axis=1, tiled=True)  17.3 us
    all_gather x1, blocking collectives, local(): all_units = lax.all_gather(pooled, 'seq', axis=0, tiled=True)  16 us
    all_gather x1, waiting for transfers between devices, local(): lax.all_gather(cross_out, 'seq', axis=0, tiled=True)  14.1 us
    dot_general x4, matrix products, fold_rows(): return jnp.dot(operand, shard_rows, preferred_element_type=jnp.float32)  12.7 us
    ppermute x1, waiting for transfers between devices, padded(): lax.ppermute(tail, axis, [(i, (i + 1) % count) for i in range(ends)])  10.7 us
  transfers between devices with their start and end apart: 7, of which 5 were waited for; matrix products, arithmetic and copies ran while one was open for 25% of the time, Pallas kernels for 0%

profile of v1, /device:TPU:1, one launch (start us, length us, event | category | flops | bytes accessed | tf_op | source)
XLA Modules:
  0.0 251.0 jit_solution(5189037876436451069)
XLA Ops:
  9.3 55.6 %all-gather.7.cloned.1.call-done = bf16[1024,3072]{1,0:T(8,128)(2,1)} async-done(((bf16[64,3072]{1,0:T(8,128)(2,1)}), bf16[1024,3072]{1,0:T(8,128)(2,1)}) %all-gather.7.cloned.1.call-update) | async-done | bytes 6291472 | tf_op jit(solution)/shard_map/all_gather | solution.py:89
  64.9 4.8 %convolution_convert_fusion = bf16[256,3072]{1,0:T(8,128)(2,1)S(1)} fusion(bf16[1024,3072]{1,0:T(8,128)(2,1)} %all-gather.7.cloned.1.call-done, bf16[256,1024]{1,0:T(8,128)(2,1)} %param.12, f32[256]{0:T(256)S(1)} %add_rsqrt_fusion.1), kind=kOutput, calls=%fused_computation.40 | convolution fusion | flops 1612185600 | bytes 8389632 | tf_op jit(solution)/shard_map/dot_general | solution.py:78
  69.8 2.7 %collective-permute-start = (bf16[256,2048]{1,0:T(8,128)(2,1)S(1)}, bf16[256,2048]{1,0:T(8,128)(2,1)}, u32[]{:S(2)}, u32[]{:S(2)}) collective-permute-start(bf16[256,2048]{1,0:T(8,128)(2,1)S(1)} %slice.45), channel_id=1, source_target_pairs={{0,1},{1,2},{2,3},{3,4},{4,5},{5,6},{6,7},{7,8},{8,9},{9,10},{10,1... | collective-permute-start | bytes 3145736 | tf_op jit(solution)/shard_map/ppermute | solution.py:26
  72.5 2.7 %collective-permute-start.1 = (bf16[256,2048]{1,0:T(8,128)(2,1)S(1)}, bf16[256,2048]{1,0:T(8,128)(2,1)}, u32[]{:S(2)}, u32[]{:S(2)}) collective-permute-start(bf16[256,2048]{1,0:T(8,128)(2,1)S(1)} %slice.45), channel_id=1, source_target_pairs={{1,0},{2,1},{3,2},{4,3},{5,4},{6,5},{7,6},{8,7},{9,8},{10,9},{11,1... | collective-permute-start | bytes 3145736 | tf_op jit(solution)/shard_map/ppermute | solution.py:28
  76.4 10.7 %collective-permute-done = bf16[256,2048]{1,0:T(8,128)(2,1)} collective-permute-done((bf16[256,2048]{1,0:T(8,128)(2,1)S(1)}, bf16[256,2048]{1,0:T(8,128)(2,1)}, u32[]{:S(2)}, u32[]{:S(2)}) %collective-permute-start) | collective-permute-done | bytes 1048608 | tf_op jit(solution)/shard_map/ppermute | solution.py:26
  87.1 6.1 %collective-permute-done.1 = bf16[256,2048]{1,0:T(8,128)(2,1)} collective-permute-done((bf16[256,2048]{1,0:T(8,128)(2,1)S(1)}, bf16[256,2048]{1,0:T(8,128)(2,1)}, u32[]{:S(2)}, u32[]{:S(2)}) %collective-permute-start.1) | collective-permute-done | bytes 1048608 | tf_op jit(solution)/shard_map/ppermute | solution.py:28
  93.2 1.7 pad_maximum_fusion
  95.2 1.6 copy.26
  97.6 33.1 %while.26 = (s32[]{:T(128)}, bf16[16,256,64]{1,2,0:T(8,128)(2,1)S(1)}, bf16[16,256,64]{1,2,0:T(8,128)(2,1)}, bf16[16,768,64]{1,2,0:T(8,128)(2,1)}, bf16[16,768,6...) while((s32[]{:T(128)}, ...), condition=%wide.region_4.5_spmd.clone, body=%wide.region_1.4_spmd.clone.sunk | while | flops 52723200 | bytes 2633565 | solution.py:73
  97.6 1.4 fusion.111
  99.7 1.4 fusion.111
  101.8 1.4 fusion.111
  103.9 1.4 fusion.111
  105.9 1.4 fusion.111
  108.0 1.4 fusion.111
  110.1 1.4 fusion.111
  112.1 1.4 fusion.111
  118.3 1.4 fusion.111
  120.4 1.4 fusion.111
  122.4 1.4 fusion.111
  124.5 1.4 fusion.111
  126.6 1.4 fusion.111
  128.6 1.4 fusion.111
  130.7 2.4 bitcast_reduce_fusion
  133.2 16.0 %all_gather.27 = bf16[128,1024]{1,0:T(8,128)(2,1)S(1)} all-gather(bf16[8,1024]{1,0:T(8,128)(2,1)S(1)} %multiply_convert_fusion.2), channel_id=1, replica_groups=mesh['doc'=32,'seq'=16] {'seq'}, dimensions={0}, use_global_device_ids=true | all-gather | bytes 278528 | tf_op jit(solution)/shard_map/all_gather | solution.py:100
  152.3 2.3 convolution_convert_fusion.1
  154.8 43.4 %all-gather.15.cloned.1.call-done = bf16[2048,1024]{1,0:T(8,128)(2,1)} async-done(((bf16[128,1024]{1,0:T(8,128)(2,1)}), bf16[2048,1024]{1,0:T(8,128)(2,1)}) %all-gather.15.cloned.1.call-update) | async-done | bytes 4194320 | tf_op jit(solution)/shard_map/all_gather | solution.py:14
  198.2 3.2 %reduce_sum.90 = bf16[128,1024]{1,0:T(8,128)(2,1)S(1)} reduce(bf16[16,128,1024]{2,1,0:T(8,128)(2,1)} %bitcast.110, bf16[]{:T(256)} %constant.77.clone.1), dimensions={0}, to_apply=%region_10.11 | reduce | flops 1966080 | bytes 4456450 | tf_op jit(solution)/shard_map/reduce_sum | solution.py:15
  202.1 17.3 %all_gather.30 = bf16[128,2048]{0,1:T(8,128)(2,1)S(1)} all-gather(bf16[128,128]{0,1:T(8,128)(2,1)S(1)} %pad_maximum_fusion.1), channel_id=1, replica_groups=mesh['doc'=32,'seq'=16] {'seq'}, dimensions={1}, use_global_device_ids=true | all-gather | bytes 557056 | tf_op jit(solution)/shard_map/all_gather | solution.py:123
  220.2 7.1 %while.25 = (s32[]{:T(128)}, bf16[16,256,64]{1,2,0:T(8,128)(2,1)S(1)}, bf16[16,256,64]{1,2,0:T(8,128)(2,1)S(1)}, bf16[16,128,64]{2,1,0:T(8,128)(2,1)S(1)}, bf16[16,128,64]{2,1,0:T(8,128)(2,1)S(1)}, /*index=5*/s32[]{:T(128)}) while((s32[]{:T(128)}, bf16[16,256,64]{1,2,0:T(8,128)(2,1)S(1)}, bf16[16,256,64]{1,2,0:T(8,128)(2,1)S(1)}, ...), condition=%wide.region_15.16_spmd, body=%wide.region_12.15_spmd.sunk | while | flops 8617474 | bytes 531525 | solution.py:73
  227.3 14.1 %all-gather.13.cloned.1.call-done = bf16[1024,1024]{1,0:T(8,128)(2,1)} async-done(((bf16[64,1024]{1,0:T(8,128)(2,1)}), bf16[1024,1024]{1,0:T(8,128)(2,1)}) %all-gather.13.cloned.1.call-update) | async-done | bytes 2097168 | tf_op jit(solution)/shard_map/all_gather | solution.py:132
  241.4 3.1 %fusion.37 = bf16[256,1024]{1,0:T(8,128)(2,1)} fusion(f32[256,1024]{1,0:T(8,128)S(1)} %get-tuple-element.163, bf16[256,1024]{0,1:T(8,128)(2,1)S(1)} %bitcast.113, bf16[1024,1024]{1,0:T(8,128)(2,1)} %all-gather.13.cloned.1.call-done), kind=kOutput, calls=%fused_computation.49 | convolution fusion | flops 537395200 | bytes 4194304 | tf_op jit(solution)/shard_map/dot_general | solution.py:78
  (133 shorter events, 29.7 us)
Async XLA Ops:
  6.5 144.0 %copy-start = (bf16[64,1024]{1,0:T(8,128)(2,1)S(1)}, bf16[64,1024]{1,0:T(8,128)(2,1)}, u32[]{:S(2)}) copy-start(bf16[64,1024]{1,0:T(8,128)(2,1)} %param.16) | copy-start | bytes 393220
  6.5 58.4 %all-gather.7.cloned.1.call-start = ((), (), s32[]{:S(2)}) async-start(), calls=%async_computation | async-start | bytes 6684672 | tf_op jit(solution)/shard_map/all_gather | solution.py:89
  7.3 123.5 %all-gather.9.cloned.1.call-start = ((), (), s32[]{:S(2)}) async-start(), calls=%async_computation.1 | async-start | bytes 2228224 | tf_op jit(solution)/shard_map/all_gather | solution.py:95
  8.0 144.3 %all-gather.11.cloned.1.call-start = ((), (), s32[]{:S(2)}) async-start(), calls=%async_computation.2 | async-start | bytes 2228224 | tf_op jit(solution)/shard_map/all_gather | solution.py:129
  69.8 17.2 %collective-permute-start = (bf16[256,2048]{1,0:T(8,128)(2,1)S(1)}, bf16[256,2048]{1,0:T(8,128)(2,1)}, u32[]{:S(2)}, u32[]{:S(2)}) collective-permute-start(bf16[256,2048]{1,0:T(8,128)(2,1)S(1)} %slice.45), channel_id=1, source_target_pairs={{0,1},{1,2},{2,3},{3,4},{4,5},{5,6},{6,7},{7,8},{8,9},{9,10},{10,1... | collective-permute-start | bytes 3145736 | tf_op jit(solution)/shard_map/ppermute | solution.py:26
  72.5 20.7 %collective-permute-start.1 = (bf16[256,2048]{1,0:T(8,128)(2,1)S(1)}, bf16[256,2048]{1,0:T(8,128)(2,1)}, u32[]{:S(2)}, u32[]{:S(2)}) collective-permute-start(bf16[256,2048]{1,0:T(8,128)(2,1)S(1)} %slice.45), channel_id=1, source_target_pairs={{1,0},{2,1},{3,2},{4,3},{5,4},{6,5},{7,6},{8,7},{9,8},{10,9},{11,1... | collective-permute-start | bytes 3145736 | tf_op jit(solution)/shard_map/ppermute | solution.py:28
  75.2 123.0 %all-gather.15.cloned.1.call-start = ((), (), s32[]{:S(2)}) async-start(), calls=%async_computation.4 | async-start | bytes 4456448 | tf_op jit(solution)/shard_map/all_gather | solution.py:14
  97.6 33.1 %copy-start.1 = (bf16[256,1024]{1,0:T(8,128)(2,1)S(1)}, bf16[256,1024]{1,0:T(8,128)(2,1)}, u32[]{:S(2)}) copy-start(bf16[256,1024]{1,0:T(8,128)(2,1)} %param.12) | copy-start | bytes 1572868
  130.7 18.6 %copy-start.2 = (bf16[1024,3,64]{0,2,1:T(8,128)(2,1)S(1)}, bf16[1024,3,64]{0,2,1:T(8,128)(2,1)}, u32[]{:S(2)}) copy-start(bf16[1024,3,64]{0,2,1:T(8,128)(2,1)} %param.15) | copy-start | bytes 1179652
  151.5 89.9 %all-gather.13.cloned.1.call-start = ((), (), s32[]{:S(2)}) async-start(), calls=%async_computation.3 | async-start | bytes 2228224 | tf_op jit(solution)/shard_map/all_gather | solution.py:132
  198.2 3.4 %copy-start.3 = (bf16[1024,2,64]{0,2,1:T(8,128)(2,1)S(1)}, bf16[1024,2,64]{0,2,1:T(8,128)(2,1)}, u32[]{:S(2)}) copy-start(bf16[1024,2,64]{0,2,1:T(8,128)(2,1)} %param.18) | copy-start | bytes 786436
Sparse Core Ops, SparseCore 0:
  9.5 55.3 all-gather.6
  67.0 41.6 all-gather.8
  110.8 41.3 all-gather.10
  154.2 43.9 all-gather.14
  200.2 41.1 all-gather.12
